TPU v7x, 256 devices: a whole 4x4x8 slice. The times are simulated.
256 devices in a mesh: tm: 4 (over x), rows: 64 (over y, z, core).
Axes of the slice: x: 4, y: 4, z: 8, core: 2. Of those that a mesh axis runs over, the one named last changes fastest.
Arguments:
- latent: bfloat16 [4, 64, 160, 512], P('tm', 'rows'), may hold values from -350 to 350, as said below
- norm_gain: float32 [512], replicated, may hold values from 0.1 to 1.9
- norm_bias: float32 [512], replicated, may hold values from -4 to 4
- conv_weight: bfloat16 [3, 3, 3, 512, 512], P(None, None, None, 'rows', 'tm'), may hold values from -0.0546875 to 0.0546875
- cotangent: bfloat16 [4, 128, 320, 512], P('tm', 'rows'), may hold values from -180 to 180
Outputs:
- latent_grad: float32 [4, 64, 160, 512], P('tm', 'rows')
- gain_grad: float32 [512], replicated
- bias_grad: float32 [512], replicated
Inputs may be any that keep to these rules, and one draw needn't show every extreme that they name: `latent`: features of the unit's input.
All inputs are finite; a program needn't handle non-finite values.
Results may differ from a plain program's by a relative error of at most 0.0003.
Values may be sent and summed in bfloat16 or wider, within the bound.
No kernel may reach another device: no remote copies, remote signals or barrier semaphores. Data moves between devices by JAX's collectives and lax.ppermute only.
A program may use at most 320 MiB of HBM per device.

v0:
```python
import jax
import jax.numpy as jnp
from jax import lax
from jax.sharding import PartitionSpec as P

GROUPS = 32


def extended(block, sides, width):
    for axis, dim in sides:
        count = lax.axis_size(axis)
        forward = [(i, i + 1) for i in range(count - 1)]
        backward = [(target, source) for source, target in forward]
        low = lax.ppermute(
            lax.slice_in_dim(block, block.shape[dim] - width, None, axis=dim), axis, forward
        )
        high = lax.ppermute(lax.slice_in_dim(block, 0, width, axis=dim), axis, backward)
        block = jnp.concatenate([low, block, high], axis=dim)
    return block


def from_behind(value, axis, steps):
    count = lax.axis_size(axis)
    first, last = (max(0, -steps), min(count, count - steps))
    return lax.ppermute(value, axis, [(source, source + steps) for source in range(first, last)])


def shifted_rows(frames, extra_frames):
    padded = jnp.pad(frames, ((0, extra_frames), (0, 0), (1, 1), (0, 0)))
    fine_rows = frames.shape[1] - 2
    return [padded[:, 2 - row_tap : 2 - row_tap + fine_rows] for row_tap in range(3)]


def tap_total(row_slabs, weights, tap_pairs, frames_out, span_cols):
    running = None
    for offset, tap_index in tap_pairs:
        for row_tap in range(3):
            source = row_slabs[row_tap][offset : offset + frames_out]
            for col_tap in range(3):
                product = lax.dot_general(
                    source,
                    weights[tap_index, row_tap, col_tap],
                    (((3,), (1,)), ((), ())),
                    preferred_element_type=jnp.float32,
                )
                piece = product[:, :, 2 - col_tap : 2 - col_tap + span_cols, :]
                running = piece if running is None else running + piece
    return running


def pool_pairs(fine_grad):
    frames, fine_rows, span_cols, channels = fine_grad.shape
    return fine_grad.reshape(frames, fine_rows // 2, 2, span_cols // 2, 2, channels).sum(
        axis=(2, 4)
    )


def block_grad(row_slabs, weights, frames_out, first_frame):
    span_cols = row_slabs[0].shape[2] - 2

    def extra_terms():
        return tap_total(row_slabs, weights, ((0, 1), (0, 0), (1, 0)), 1, span_cols)

    def no_terms():
        return jnp.zeros((1, row_slabs[0].shape[1], span_cols, weights.shape[3]), jnp.float32)

    main_part = tap_total(row_slabs, weights, ((0, 2), (1, 1), (2, 0)), frames_out, span_cols)
    main_part = main_part + lax.cond(first_frame, extra_terms, no_terms)
    return pool_pairs(main_part)


def on_device(latent, norm_gain, norm_bias, conv_weight, cotangent):
    frames_all = lax.axis_size("tm")
    rows_all = lax.axis_size("rows")
    low_rows = latent.shape[1]
    low_cols = latent.shape[2]
    channels = latent.shape[3]
    per_group = channels // GROUPS
    cell_count = frames_all * rows_all * low_rows * low_cols
    rimmed = extended(cotangent, (("rows", 1),), 1)
    following = from_behind(rimmed, "tm", -1)
    further = from_behind(rimmed, "tm", -2)
    stacked = jnp.concatenate([rimmed, following, further], axis=0)
    weight_wide = lax.all_gather(conv_weight, "tm", axis=4, tiled=True)
    weight_full = lax.all_gather(weight_wide, "rows", axis=3, tiled=True)
    up_grad = block_grad(shifted_rows(stacked, 0), weight_full, 1, lax.axis_index("tm") == 0)
    features = latent.astype(jnp.float32)
    sum_x = jnp.sum(features, axis=(0, 1, 2))
    sum_sq = jnp.sum(features * features, axis=(0, 1, 2))
    total_x, total_sq = lax.psum((sum_x, sum_sq), ("tm", "rows"))
    group_x = total_x.reshape(GROUPS, per_group).sum(axis=1)
    group_sq = total_sq.reshape(GROUPS, per_group).sum(axis=1)
    group_mean = group_x / (cell_count * per_group)
    group_var = group_sq / (cell_count * per_group) - group_mean * group_mean
    inv_std = lax.rsqrt(group_var + 1e-06)
    mean_chan = jnp.repeat(group_mean, per_group)
    inv_chan = jnp.repeat(inv_std, per_group)
    normed = (features - mean_chan) * inv_chan
    pre = normed * norm_gain + norm_bias
    sigmoid_pre = jax.nn.sigmoid(pre)
    act_grad = up_grad * sigmoid_pre * (1.0 + pre * (1.0 - sigmoid_pre))
    sum_act, sum_scaled = lax.psum(
        (jnp.sum(act_grad, axis=(0, 1, 2)), jnp.sum(act_grad * normed, axis=(0, 1, 2))),
        ("tm", "rows"),
    )
    gain_grad = sum_scaled / cell_count
    bias_grad = sum_act / cell_count
    mean_q = (norm_gain * sum_act).reshape(GROUPS, per_group).sum(axis=1) / (cell_count * per_group)
    mean_qn = (norm_gain * sum_scaled).reshape(GROUPS, per_group).sum(axis=1) / (
        cell_count * per_group
    )
    latent_grad = inv_chan * (
        act_grad * norm_gain
        - jnp.repeat(mean_q, per_group)
        - normed * jnp.repeat(mean_qn, per_group)
    )
    return (latent_grad, gain_grad, bias_grad)


def solution(mesh):
    placed = (
        P("tm", "rows", None, None),
        P(),
        P(),
        P(None, None, None, "rows", "tm"),
        P("tm", "rows", None, None),
    )
    return jax.shard_map(
        on_device,
        mesh=mesh,
        in_specs=placed,
        out_specs=(P("tm", "rows", None, None), P(), P()),
        check_vma=False,
    )
```

profile of v0, /device:TPU:1, one launch (start us, length us, event | category | flops | bytes accessed | tf_op | source)
XLA Modules:
  0.0 354.6 jit_solution(4041163253013684087)
XLA Ops:
  7.2 11.7 %all_gather.6 = bf16[3,3,3,8,512]{4,3,2,1,0:T(8,128)(2,1)} all-gather(bf16[3,3,3,8,128]{4,3,2,1,0:T(8,128)(2,1)} %param.10), channel_id=1, replica_groups=mesh['tm'=4,'rows'=64] {'tm'}, dimensions={4}, use_global_device_ids=true | all-gather | bytes 276480 | tf_op jit(solution)/shard_map/all_gather | solution.py:84
  20.1 6.2 %collective-permute-start = (bf16[1,1,320,512]{3,2,1,0:T(8,128)(2,1)S(1)}, bf16[1,1,320,512]{3,2,1,0:T(8,128)(2,1)S(1)}, u32[]{:S(2)}, u32[]{:S(2)}) collective-permute-start(bf16[1,1,320,512]{3,2,1,0:T(8,128)(2,1)S(1)} %get-tuple-element.27), channel_id=1, source_target_pairs={{0,1},{1,2},{2,3},{3,4},{4,5},{5,6},{6,7},{7,8},{8,9},{9,10},{10,1... | collective-permute-start | bytes 983048 | tf_op jit(solution)/shard_map/ppermute | solution.py:14
  26.3 1.9 collective-permute-start.1
  28.2 2.1 collective-permute-done
  30.4 4.3 %collective-permute-done.1 = bf16[1,1,320,512]{3,2,1,0:T(8,128)(2,1)S(1)} collective-permute-done((bf16[1,1,320,512]{3,2,1,0:T(8,128)(2,1)S(1)}, bf16[1,1,320,512]{3,2,1,0:T(8,128)(2,1)S(1)}, u32[]{:S(2)}, u32[]{:S(2)}) %collective-permute-start.1) | collective-permute-done | bytes 327712 | tf_op jit(solution)/shard_map/ppermute | solution.py:17
  37.6 129.7 %all-reduce.2 = (f32[32,16]{1,0:T(8,128)S(1)}, f32[32,16]{1,0:T(8,128)S(1)}) all-reduce(f32[32,16]{1,0:T(8,128)S(1)} %reshape.178, f32[32,16]{1,0:T(8,128)S(1)} %reshape.177), channel_id=1, replica_groups=mesh['tm'=4,'rows'=64] {'tm','rows'}, use_global_device_ids=true, to_apply=%region_4.5 | all-reduce | flops 1024 | bytes 8192 | tf_op jit(solution)/shard_map/psum | solution.py:90
  167.8 3.9 %fusion.113 = bf16[3,4,322,512]{3,2,1,0:T(8,128)(2,1)} fusion(bf16[1,4,320,512]{3,2,1,0:T(8,128)(2,1)} %collective-permute-done.3, bf16[1,4,320,512]{3,2,1,0:T(8,128)(2,1)} %collective-permute-done.2, bf16[1,4,320,512]{3,2,1,0:T(8,128)(2,1)S(1)} %constant_dynamic-update-slice_fusion), kind=kLoop, calls=%fused_computation.168 | loop fusion | flops 23740416 | bytes 7888896 | tf_op jit(solution)/shard_map/concatenate | solution.py:83
  171.7 48.1 %conditional.1 = (f32[1,2,320,512]{3,2,1,0:T(8,128)}) conditional(s32[]{:T(128)} %convert_element_type.9, () %tuple.14, (bf16[3,4,322,512]{3,2,1,0:T(8,128)(2,1)}, bf16[3,3,3,512,512]{4,3,2,1,0:T(8,128)(2,1)}) %tuple.15), branch_computations={%region_6.7_spmd, %region_7.8_spmd} | conditional | flops 9124839424 | bytes 177053760 | solution.py:68
  171.7 1.9 convolution_bitcast_fusion.15
  173.6 1.8 convolution_bitcast_fusion.16
  175.5 1.7 convolution_bitcast_fusion.17
  177.2 2.0 convolution_bitcast_fusion.24
  179.2 2.1 convolution_bitcast_fusion.25
  189.4 1.6 convolution_bitcast_fusion.19
  191.0 1.6 convolution_bitcast_fusion.6
  192.7 1.6 convolution_bitcast_fusion.7
  194.3 1.7 convolution_bitcast_fusion.3
  195.9 1.6 convolution_bitcast_fusion.4
  197.5 1.6 convolution_bitcast_fusion
  199.2 1.6 convolution_bitcast_fusion.1
  200.8 1.6 convolution_bitcast_fusion.2
  202.4 1.7 convolution_bitcast_fusion.5
  204.1 1.7 convolution_bitcast_fusion.8
  205.8 1.7 convolution_bitcast_fusion.20
  207.5 1.6 convolution_bitcast_fusion.23
  209.1 1.6 convolution_bitcast_fusion.26
  210.7 9.0 %slice_add_fusion = f32[1,2,320,512]{3,2,1,0:T(8,128)} fusion(f32[1,2,322,512]{3,2,1,0:T(8,128)} %convolution_bitcast_fusion, f32[1,2,322,512]{3,2,1,0:T(8,128)} %convolution_bitcast_fusion.1, f32[1,2,322,512]{3,2,1,0:T(8,128)} %convolution_bitcast_fusion.2, f32[1,2,322,512]{3,2,1,0:T(8,128)} %convolution_bitcast_fusion.3, ...), kind=kLoop, calls=%fused_computation.27 | loop fusion | flops 8519680 | bytes 36700160 | tf_op jit(solution)/shard_map/cond/branch_1_fun/add | solution.py:47
  219.8 1.9 convolution_bitcast_fusion.28
  221.7 1.8 convolution_bitcast_fusion.27
  223.6 1.7 convolution_bitcast_fusion.31
  225.3 2.0 convolution_bitcast_fusion.30
  227.3 2.1 convolution_bitcast_fusion.34
  237.0 1.7 convolution_bitcast_fusion.45
  238.7 1.7 convolution_bitcast_fusion.49
  240.4 1.6 convolution_bitcast_fusion.48
  242.0 1.6 convolution_bitcast_fusion.52
  243.6 1.6 convolution_bitcast_fusion.51
  245.2 1.6 convolution_bitcast_fusion.29
  246.9 1.6 convolution_bitcast_fusion.32
  248.5 1.6 convolution_bitcast_fusion.35
  250.1 1.6 convolution_bitcast_fusion.38
  251.7 1.7 convolution_bitcast_fusion.41
  253.4 1.6 convolution_bitcast_fusion.44
  255.0 1.6 convolution_bitcast_fusion.47
  256.6 1.6 convolution_bitcast_fusion.50
  258.2 1.7 convolution_bitcast_fusion.53
  259.9 10.1 %fusion.115 = f32[320,512]{1,0:T(8,128)} fusion(f32[1,2,320,512]{3,2,1,0:T(8,128)} %get-tuple-element.34, f32[1,2,322,512]{3,2,1,0:T(8,128)S(1)} %convolution_bitcast_fusion.27, f32[1,2,322,512]{3,2,1,0:T(8,128)S(1)} %convolution_bitcast_fusion.28, f32[1,2,322,512]{3,2,1,0:T(8,128)} %convolution_bitcast_fusion.29, ...), kind=kLoop, calls=%fused_computation.198 | loop fusion | flops 9011200 | bytes 37355520 | tf_op jit(solution)/shard_map/reduce_sum | solution.py:53
  272.5 73.1 %all-reduce.1 = (f32[512]{0:T(512)S(1)}, f32[512]{0:T(512)S(1)}) all-reduce(f32[512]{0:T(512)S(1)} %get-tuple-element.18, f32[512]{0:T(512)S(1)} %get-tuple-element.17), channel_id=1, replica_groups=mesh['tm'=4,'rows'=64] {'tm','rows'}, use_global_device_ids=true, to_apply=%region_14.15 | all-reduce | flops 1024 | bytes 8192 | tf_op jit(solution)/shard_map/psum | solution.py:102
  (69 shorter events, 24.7 us)
Async XLA Ops:
  7.2 23.2 %copy-start.4 = (bf16[1,2,320,512]{3,2,1,0:T(8,128)(2,1)S(1)}, bf16[1,2,320,512]{3,2,1,0:T(8,128)(2,1)}, u32[]{:S(2)}) copy-start(bf16[1,2,320,512]{3,2,1,0:T(8,128)(2,1)} %param.11) | copy-start | bytes 1966084
  7.2 164.5 %all-gather.2.cloned.1.call-start = ((), (), s32[]{:S(2)}) async-start(), calls=%async_computation | async-start | bytes 14376960 | tf_op jit(solution)/shard_map/all_gather | solution.py:85
  20.0 17.3 %copy-start.5 = (bf16[1,1,160,512]{3,2,1,0:T(8,128)(2,1)S(1)}, bf16[1,1,160,512]{3,2,1,0:T(8,128)(2,1)}, u32[]{:S(2)}) copy-start(bf16[1,1,160,512]{3,2,1,0:T(8,128)(2,1)} %param.7) | copy-start | bytes 491524
  20.1 10.2 %collective-permute-start = (bf16[1,1,320,512]{3,2,1,0:T(8,128)(2,1)S(1)}, bf16[1,1,320,512]{3,2,1,0:T(8,128)(2,1)S(1)}, u32[]{:S(2)}, u32[]{:S(2)}) collective-permute-start(bf16[1,1,320,512]{3,2,1,0:T(8,128)(2,1)S(1)} %get-tuple-element.27), channel_id=1, source_target_pairs={{0,1},{1,2},{2,3},{3,4},{4,5},{5,6},{6,7},{7,8},{8,9},{9,10},{10,1... | collective-permute-start | bytes 983048 | tf_op jit(solution)/shard_map/ppermute | solution.py:14
  26.3 8.4 %collective-permute-start.1 = (bf16[1,1,320,512]{3,2,1,0:T(8,128)(2,1)S(1)}, bf16[1,1,320,512]{3,2,1,0:T(8,128)(2,1)S(1)}, u32[]{:S(2)}, u32[]{:S(2)}) collective-permute-start(bf16[1,1,320,512]{3,2,1,0:T(8,128)(2,1)S(1)} %get-tuple-element.26), channel_id=1, source_target_pairs={{1,0},{2,1},{3,2},{4,3},{5,4},{6,5},{7,6},{8,7},{9,8},{10,9},{11,1... | collective-permute-start | bytes 983048 | tf_op jit(solution)/shard_map/ppermute | solution.py:17
  34.7 133.1 %collective-permute-start.3 = (bf16[1,4,320,512]{3,2,1,0:T(8,128)(2,1)S(1)}, bf16[1,4,320,512]{3,2,1,0:T(8,128)(2,1)}, u32[]{:S(2)}, u32[]{:S(2)}) collective-permute-start(bf16[1,4,320,512]{3,2,1,0:T(8,128)(2,1)S(1)} %constant_dynamic-update-slice_fusion), channel_id=1, source_target_pairs={{128,0},{192,64},{129,1},{193,65},{130,2},{194,66},{131,3},{195,67... | collective-permute-start | bytes 3932168 | tf_op jit(solution)/shard_map/ppermute | solution.py:25
  36.0 131.8 %collective-permute-start.2 = (bf16[1,4,320,512]{3,2,1,0:T(8,128)(2,1)S(1)}, bf16[1,4,320,512]{3,2,1,0:T(8,128)(2,1)}, u32[]{:S(2)}, u32[]{:S(2)}) collective-permute-start(bf16[1,4,320,512]{3,2,1,0:T(8,128)(2,1)S(1)} %constant_dynamic-update-slice_fusion), channel_id=1, source_target_pairs={{64,0},{128,64},{192,128},{65,1},{129,65},{193,129},{66,2},{130,66... | collective-permute-start | bytes 3932168 | tf_op jit(solution)/shard_map/ppermute | solution.py:25
  171.7 3.7 %copy-start.1 = (bf16[3,4,322,512]{3,2,1,0:T(8,128)(2,1)S(1)}, bf16[3,4,322,512]{3,2,1,0:T(8,128)(2,1)}, u32[]{:S(2)}) copy-start(bf16[3,4,322,512]{3,2,1,0:T(8,128)(2,1)} %get-tuple-element.12) | copy-start | bytes 11870212 | tf_op jit(solution)/shard_map/cond
  175.4 10.7 %copy-start.3 = (bf16[3,3,3,512,512]{4,3,2,1,0:T(8,128)(2,1)S(1)}, bf16[3,3,3,512,512]{4,3,2,1,0:T(8,128)(2,1)}, u32[]{:S(2)}) copy-start(bf16[3,3,3,512,512]{4,3,2,1,0:T(8,128)(2,1)} %get-tuple-element.13) | copy-start | bytes 42467332 | tf_op jit(solution)/shard_map/cond
  219.8 3.7 %copy-start = (bf16[3,4,322,512]{3,2,1,0:T(8,128)(2,1)S(1)}, bf16[3,4,322,512]{3,2,1,0:T(8,128)(2,1)}, u32[]{:S(2)}) copy-start(bf16[3,4,322,512]{3,2,1,0:T(8,128)(2,1)} %fusion.113) | copy-start | bytes 11870212
  223.5 10.7 %copy-start.2 = (bf16[3,3,3,512,512]{4,3,2,1,0:T(8,128)(2,1)S(1)}, bf16[3,3,3,512,512]{4,3,2,1,0:T(8,128)(2,1)}, u32[]{:S(2)}) copy-start(bf16[3,3,3,512,512]{4,3,2,1,0:T(8,128)(2,1)} %all-gather.2.cloned.1.call-done) | copy-start | bytes 42467332
  270.0 2.3 copy-start.6
  270.0 2.3 copy-start.7
Sparse Core Ops, SparseCore 0:
  19.0 105.3 all-gather.1
where the time goes:
time: 355 us
  blocking collectives  214 us (60%)
  matrix products  78.8 us (22%)
  other arithmetic  26 us (7%)
  between operations  14.3 us (4%)
  starting transfers between devices  10.8 us (3%)
  waiting for transfers between devices  6.41 us (2%)
  local copies, waits for them, and re-layouts  3.66 us (1%)
    psum x1, blocking collectives, on_device(): total_x, total_sq = lax.psum((sum_x, sum_sq), ('tm', 'rows'))  130 us
    dot_general x54, matrix products, tap_total(): lax.dot_general(source, weights[tap_index, row_tap, col_tap], (((3,), (1,...  78.8 us
    psum x1, blocking collectives, on_device(): lax.psum((jnp.sum(act_grad, axis=(0, 1, 2)), jnp.sum(act_grad * normed, a...  73.1 us
    all_gather x1, blocking collectives, on_device(): weight_wide = lax.all_gather(conv_weight, 'tm', axis=4, tiled=True)  11.7 us
    reduce_sum x2, other arithmetic, pool_pairs(): fine_grad.reshape(frames, fine_rows // 2, 2, span_cols // 2, 2, channels)  10.9 us
    add x1, other arithmetic, tap_total(): running = piece if running is None else running + piece  9.05 us
  transfers between devices with their start and end apart: 5, of which 2 were waited for; matrix products, arithmetic and copies ran while one was open for 2% of the time, Pallas kernels for 0%

commit v1 on v0

--- a/solution.py
+++ b/solution.py
@@ -82,7 +82,9 @@
     further = from_behind(rimmed, "tm", -2)
     stacked = jnp.concatenate([rimmed, following, further], axis=0)
     weight_wide = lax.all_gather(conv_weight, "tm", axis=4, tiled=True)
-    weight_full = lax.all_gather(weight_wide, "rows", axis=3, tiled=True)
+    weight_full = jnp.concatenate(
+        lax.all_to_all(jnp.stack([weight_wide] * lax.axis_size("rows")), "rows", 0, 0), axis=3
+    )
     up_grad = block_grad(shifted_rows(stacked, 0), weight_full, 1, lax.axis_index("tm") == 0)
     features = latent.astype(jnp.float32)
     sum_x = jnp.sum(features, axis=(0, 1, 2))

time: 355 us -> 658 us (1.85)
  waiting for transfers between devices: 6.41 us -> 304 us
  between operations: 14.3 us -> 0.88 us
  starting transfers between devices: 10.8 us -> 22.5 us
  local copies, waits for them, and re-layouts: 3.66 us -> 14.5 us
    ppermute x1, waiting for transfers between devices: 2.07 us -> 302 us  [extended(): lax.ppermute(lax.slice_in_dim(block, block.shape[dim] - width, None, axis...]
    all_to_all x0 -> x1, starting transfers between devices: none -> 14.3 us  [on_device(): lax.all_to_all(jnp.stack([weight_wide] * lax.axis_size('rows')), 'rows',...]
    reshape x0 -> x1, local copies, waits for them, and re-layouts: none -> 7.04 us  [on_device(): jnp.concatenate(lax.all_to_all(jnp.stack([weight_wide] * lax.axis_size('r...]
  transfers between devices with their start and end apart: 5 -> 5, of which waited for: 2 -> 2; matrix products, arithmetic and copies ran while one was open for 2% -> 1% of each run, Pallas kernels for 0% -> 0%
where the time goes in v1:
time: 658 us
  waiting for transfers between devices  304 us (46%)
  blocking collectives  212 us (32%)
  matrix products  74.1 us (11%)
  other arithmetic  30.3 us (5%)
  starting transfers between devices  22.5 us (3%)
  local copies, waits for them, and re-layouts  14.5 us (2%)
    ppermute x1, waiting for transfers between devices, extended(): lax.ppermute(lax.slice_in_dim(block, block.shape[dim] - width, None, axis...  302 us
    psum x1, blocking collectives, on_device(): total_x, total_sq = lax.psum((sum_x, sum_sq), ('tm', 'rows'))  127 us
    dot_general x54, matrix products, tap_total(): lax.dot_general(source, weights[tap_index, row_tap, col_tap], (((3,), (1,...  74.1 us
    psum x1, blocking collectives, on_device(): lax.psum((jnp.sum(act_grad, axis=(0, 1, 2)), jnp.sum(act_grad * normed, a...  73.4 us
    all_to_all x1, starting transfers between devices, on_device(): lax.all_to_all(jnp.stack([weight_wide] * lax.axis_size('rows')), 'rows',...  14.3 us
    reduce_sum x2, other arithmetic, pool_pairs(): fine_grad.reshape(frames, fine_rows // 2, 2, span_cols // 2, 2, channels)  14.1 us
  transfers between devices with their start and end apart: 5, of which 2 were waited for; matrix products, arithmetic and copies ran while one was open for 1% of the time, Pallas kernels for 0%

profile of v1, /device:TPU:1, one launch (start us, length us, event | category | flops | bytes accessed | tf_op | source)
XLA Modules:
  0.0 657.9 jit_solution(5840074737089318877)
XLA Ops:
  0.6 11.1 %all_gather.3 = bf16[3,3,3,8,512]{4,3,2,1,0:T(8,128)(2,1)S(1)} all-gather(bf16[3,3,3,8,128]{4,3,2,1,0:T(8,128)(2,1)} %param.10), channel_id=1, replica_groups=mesh['tm'=4,'rows'=64] {'tm'}, dimensions={4}, use_global_device_ids=true | all-gather | bytes 276480 | tf_op jit(solution)/shard_map/all_gather | solution.py:84
  11.8 6.0 stack.2
  17.8 14.3 %all-to-all-start = ((bf16[64,3,3,3,8,512]{5,4,3,2,1,0:T(8,128)(2,1)}), bf16[64,3,3,3,8,512]{5,4,3,2,1,0:T(8,128)(2,1)}, u32[]{:S(2)}, u32[]{:S(2)}) async-start(bf16[64,3,3,3,8,512]{5,4,3,2,1,0:T(8,128)(2,1)} %stack.2), calls=%async_computation | async-start | bytes 28311552 | tf_op jit(solution)/shard_map/all_to_all | solution.py:86
  32.2 3.7 collective-permute-start
  35.9 1.9 collective-permute-start.1
  37.8 301.6 %collective-permute-done = bf16[1,1,320,512]{3,2,1,0:T(8,128)(2,1)S(1)} collective-permute-done((bf16[1,1,320,512]{3,2,1,0:T(8,128)(2,1)S(1)}, bf16[1,1,320,512]{3,2,1,0:T(8,128)(2,1)S(1)}, u32[]{:S(2)}, u32[]{:S(2)}) %collective-permute-start) | collective-permute-done | bytes 327712 | tf_op jit(solution)/shard_map/ppermute | solution.py:14
  339.5 2.1 collective-permute-done.1
  344.4 127.1 %all-reduce.2 = (f32[32,16]{1,0:T(8,128)S(1)}, f32[32,16]{1,0:T(8,128)S(1)}) all-reduce(f32[32,16]{1,0:T(8,128)S(1)} %reshape.186, f32[32,16]{1,0:T(8,128)S(1)} %reshape.185), channel_id=1, replica_groups=mesh['tm'=4,'rows'=64] {'tm','rows'}, use_global_device_ids=true, to_apply=%region_4.5 | all-reduce | flops 1024 | bytes 8192 | tf_op jit(solution)/shard_map/psum | solution.py:92
  472.1 3.7 fusion.113
  475.8 7.0 %copy_bitcast_fusion = bf16[3,3,3,512,512]{4,3,2,1,0:T(8,128)(2,1)S(1)} fusion(bf16[64,3,3,3,8,512]{5,4,3,2,1,0:T(8,128)(2,1)} %all-to-all-done), kind=kLoop, calls=%fused_computation.161 | loop fusion | bytes 28311552 | tf_op jit(solution)/shard_map/reshape | solution.py:85
  484.0 1.6 convolution_bitcast_fusion.29
  485.6 1.6 convolution_bitcast_fusion.30
  488.8 1.6 convolution_bitcast_fusion.32
  490.5 1.7 convolution_bitcast_fusion.33
  492.1 1.6 convolution_bitcast_fusion.34
  493.7 1.7 convolution_bitcast_fusion.35
  497.0 1.6 convolution_bitcast_fusion.37
  498.7 1.7 convolution_bitcast_fusion.38
  500.3 1.6 convolution_bitcast_fusion.39
  502.0 1.6 convolution_bitcast_fusion.40
  503.6 1.6 convolution_bitcast_fusion.41
  505.2 1.6 convolution_bitcast_fusion.42
  506.9 1.6 convolution_bitcast_fusion.43
  508.5 1.6 convolution_bitcast_fusion.44
  510.1 1.7 convolution_bitcast_fusion.45
  511.8 1.7 convolution_bitcast_fusion.46
  513.4 1.7 convolution_bitcast_fusion.47
  515.1 1.7 convolution_bitcast_fusion.48
  516.8 1.6 convolution_bitcast_fusion.49
  518.4 1.6 convolution_bitcast_fusion.50
  520.1 1.7 convolution_bitcast_fusion.51
  521.7 1.6 convolution_bitcast_fusion.52
  523.3 1.7 convolution_bitcast_fusion.53
  525.0 42.6 %conditional.1 = (f32[1,2,320,512]{3,2,1,0:T(8,128)}) conditional(s32[]{:T(128)} %convert_element_type.9, () %tuple.14, (bf16[3,4,322,512]{3,2,1,0:T(8,128)(2,1)S(1)}, bf16[3,3,3,512,512]{4,3,2,1,0:T(8,128)(2,1)S(1)}) %tuple.27), branch_computations={%region_6.7_spmd, %region_7.8_spmd} | conditional | flops 9124839424 | bytes 104603656 | solution.py:68
  531.0 1.6 convolution_bitcast_fusion.10
  532.7 1.7 convolution_bitcast_fusion.11
  534.3 1.6 convolution_bitcast_fusion.18
  535.9 1.7 convolution_bitcast_fusion.19
  537.6 1.6 convolution_bitcast_fusion.6
  539.2 1.7 convolution_bitcast_fusion.7
  540.9 1.6 convolution_bitcast_fusion.3
  544.2 1.6 convolution_bitcast_fusion
  547.4 1.6 convolution_bitcast_fusion.2
  552.2 1.6 convolution_bitcast_fusion.20
  555.5 1.7 convolution_bitcast_fusion.26
  557.1 10.2 %slice_add_fusion = f32[1,2,320,512]{3,2,1,0:T(8,128)} fusion(f32[1,2,322,512]{3,2,1,0:T(8,128)} %convolution_bitcast_fusion, f32[1,2,322,512]{3,2,1,0:T(8,128)} %convolution_bitcast_fusion.1, f32[1,2,322,512]{3,2,1,0:T(8,128)} %convolution_bitcast_fusion.2, f32[1,2,322,512]{3,2,1,0:T(8,128)} %convolution_bitcast_fusion.3, ...), kind=kLoop, calls=%fused_computation.27 | loop fusion | flops 8519680 | bytes 36700160 | tf_op jit(solution)/shard_map/cond/branch_1_fun/add | solution.py:47
  567.6 13.4 %fusion.115 = f32[320,512]{1,0:T(8,128)S(1)} fusion(f32[1,2,320,512]{3,2,1,0:T(8,128)} %get-tuple-element.34, f32[1,2,322,512]{3,2,1,0:T(8,128)S(1)} %convolution_bitcast_fusion.27, f32[1,2,322,512]{3,2,1,0:T(8,128)S(1)} %convolution_bitcast_fusion.28, f32[1,2,322,512]{3,2,1,0:T(8,128)} %convolution_bitcast_fusion.29, ...), kind=kLoop, calls=%fused_computation.199 | loop fusion | flops 9011200 | bytes 37355520 | tf_op jit(solution)/shard_map/reduce_sum | solution.py:53
  582.4 73.4 %all-reduce.1 = (f32[512]{0:T(512)S(1)}, f32[512]{0:T(512)S(1)}) all-reduce(f32[512]{0:T(512)S(1)} %get-tuple-element.18, f32[512]{0:T(512)S(1)} %get-tuple-element.17), channel_id=1, replica_groups=mesh['tm'=4,'rows'=64] {'tm','rows'}, use_global_device_ids=true, to_apply=%region_14.15 | all-reduce | flops 1024 | bytes 8192 | tf_op jit(solution)/shard_map/psum | solution.py:104
  (64 shorter events, 25.2 us)
Async XLA Ops:
  17.8 14.3 %copy-start.1 = (bf16[1,2,320,512]{3,2,1,0:T(8,128)(2,1)S(1)}, bf16[1,2,320,512]{3,2,1,0:T(8,128)(2,1)}, u32[]{:S(2)}) copy-start(bf16[1,2,320,512]{3,2,1,0:T(8,128)(2,1)} %param.11) | copy-start | bytes 1966084
  17.8 458.0 %all-to-all-start = ((bf16[64,3,3,3,8,512]{5,4,3,2,1,0:T(8,128)(2,1)}), bf16[64,3,3,3,8,512]{5,4,3,2,1,0:T(8,128)(2,1)}, u32[]{:S(2)}, u32[]{:S(2)}) async-start(bf16[64,3,3,3,8,512]{5,4,3,2,1,0:T(8,128)(2,1)} %stack.2), calls=%async_computation | async-start | bytes 28311552 | tf_op jit(solution)/shard_map/all_to_all | solution.py:86
  32.2 312.0 %copy-start.2 = (bf16[1,1,160,512]{3,2,1,0:T(8,128)(2,1)S(1)}, bf16[1,1,160,512]{3,2,1,0:T(8,128)(2,1)}, u32[]{:S(2)}) copy-start(bf16[1,1,160,512]{3,2,1,0:T(8,128)(2,1)} %param.7) | copy-start | bytes 491524
  32.2 307.2 %collective-permute-start = (bf16[1,1,320,512]{3,2,1,0:T(8,128)(2,1)S(1)}, bf16[1,1,320,512]{3,2,1,0:T(8,128)(2,1)S(1)}, u32[]{:S(2)}, u32[]{:S(2)}) collective-permute-start(bf16[1,1,320,512]{3,2,1,0:T(8,128)(2,1)S(1)} %get-tuple-element.27), channel_id=1, source_target_pairs={{0,1},{1,2},{2,3},{3,4},{4,5},{5,6},{6,7},{7,8},{8,9},{9,10},{10,1... | collective-permute-start | bytes 983048 | tf_op jit(solution)/shard_map/ppermute | solution.py:14
  35.9 305.7 %collective-permute-start.1 = (bf16[1,1,320,512]{3,2,1,0:T(8,128)(2,1)S(1)}, bf16[1,1,320,512]{3,2,1,0:T(8,128)(2,1)S(1)}, u32[]{:S(2)}, u32[]{:S(2)}) collective-permute-start(bf16[1,1,320,512]{3,2,1,0:T(8,128)(2,1)S(1)} %get-tuple-element.26), channel_id=1, source_target_pairs={{1,0},{2,1},{3,2},{4,3},{5,4},{6,5},{7,6},{8,7},{9,8},{10,9},{11,1... | collective-permute-start | bytes 983048 | tf_op jit(solution)/shard_map/ppermute | solution.py:17
  341.6 130.5 %collective-permute-start.3 = (bf16[1,4,320,512]{3,2,1,0:T(8,128)(2,1)S(1)}, bf16[1,4,320,512]{3,2,1,0:T(8,128)(2,1)S(1)}, u32[]{:S(2)}, u32[]{:S(2)}) collective-permute-start(bf16[1,4,320,512]{3,2,1,0:T(8,128)(2,1)S(1)} %constant_dynamic-update-slice_fusion), channel_id=1, source_target_pairs={{128,0},{192,64},{129,1},{193,65},{130,2},{194,66},{131,3},{195,67... | collective-permute-start | bytes 3932168 | tf_op jit(solution)/shard_map/ppermute | solution.py:25
  342.9 129.2 %collective-permute-start.2 = (bf16[1,4,320,512]{3,2,1,0:T(8,128)(2,1)S(1)}, bf16[1,4,320,512]{3,2,1,0:T(8,128)(2,1)}, u32[]{:S(2)}, u32[]{:S(2)}) collective-permute-start(bf16[1,4,320,512]{3,2,1,0:T(8,128)(2,1)S(1)} %constant_dynamic-update-slice_fusion), channel_id=1, source_target_pairs={{64,0},{128,64},{192,128},{65,1},{129,65},{193,129},{66,2},{130,66... | collective-permute-start | bytes 3932168 | tf_op jit(solution)/shard_map/ppermute | solution.py:25
  475.8 7.0 %copy-start = (bf16[3,4,322,512]{3,2,1,0:T(8,128)(2,1)S(1)}, bf16[3,4,322,512]{3,2,1,0:T(8,128)(2,1)}, u32[]{:S(2)}) copy-start(bf16[3,4,322,512]{3,2,1,0:T(8,128)(2,1)} %fusion.113) | copy-start | bytes 11870212
  581.0 1.2 copy-start.3
  581.0 1.2 copy-start.4
